TPU v7x, 32 devices: a whole 2x2x4 slice. The times are simulated.
32 devices in a mesh: gx: 2 (over x), gy: 1, gz: 16 (over z, y, core).
Axes of the slice: x: 2, y: 2, z: 4, core: 2. Of those that a mesh axis runs over, the one named last changes fastest.
Arguments:
- volume: bfloat16 [32, 64, 8, 256], P(None, 'gx', 'gy', 'gz'), may hold values from -6 to 6
- weight_a: bfloat16 [3, 3, 3, 32, 64], replicated, may hold values from -0.21875 to 0.21875
- bias_a: float32 [64], replicated, may hold values from -3 to 3
- weight_b: bfloat16 [3, 3, 3, 64, 128], replicated, may hold values from -0.15625 to 0.15625
- bias_b: float32 [128], replicated, may hold values from -3 to 3
- cotangent: bfloat16 [128, 32, 4, 128], P(None, ('gx', 'gz'), 'gy'), may hold values from -24 to 24
Outputs:
- features: bfloat16 [128, 32, 4, 128], P(None, ('gx', 'gz'), 'gy')
- grad_input: bfloat16 [32, 64, 8, 256], P(None, 'gx', 'gy', 'gz')
- grad_weight_a: float32 [3, 3, 3, 32, 64], replicated
- grad_bias_a: float32 [64], replicated
- grad_weight_b: float32 [3, 3, 3, 64, 128], replicated
- grad_bias_b: float32 [128], replicated
All inputs are finite; a program needn't handle non-finite values.
Results may differ from a plain program's by a relative error of at most 0.012.
Values may be sent and summed in bfloat16 or wider, within the bound.
A program may use at most 128 MiB of HBM per device.

v0:
```python
import math

import jax
import jax.numpy as jnp
from jax import lax
from jax.sharding import PartitionSpec as P


def padded_2(block, sides, width):
    for axis, dim in sides:
        count = lax.axis_size(axis)
        forward = [(i, i + 1) for i in range(count - 1)]
        backward = [(target, source) for source, target in forward]
        low = lax.ppermute(
            lax.slice_in_dim(block, block.shape[dim] - width, None, axis=dim), axis, forward
        )
        high = lax.ppermute(lax.slice_in_dim(block, 0, width, axis=dim), axis, backward)
        block = jnp.concatenate([low, block, high], axis=dim)
    return block


def activate(value):
    return value * jax.nn.sigmoid(value)


def slope_of(value):
    sigma = jax.nn.sigmoid(value)
    return sigma + value * sigma * (1.0 - sigma)


def conv_valid(padded, weight):
    result = lax.conv_general_dilated(
        padded[None],
        weight,
        (1, 1, 1),
        "VALID",
        dimension_numbers=("NCDHW", "DHWIO", "NCDHW"),
        preferred_element_type=jnp.float32,
    )
    return result[0]


def flipped(weight):
    return jnp.transpose(weight[::-1, ::-1, ::-1], (0, 1, 2, 4, 3))


def average_pool(field):
    shape = field.shape
    split = field.reshape(shape[0], shape[1] // 2, 2, shape[2] // 2, 2, shape[3] // 2, 2)
    return jnp.sum(split, axis=(2, 4, 6)) * 0.125


def spread_back(field):
    shape = field.shape
    larger = jnp.broadcast_to(
        field[:, :, None, :, None, :, None], (shape[0], shape[1], 2, shape[2], 2, shape[3], 2)
    )
    return larger.reshape(shape[0], 2 * shape[1], 2 * shape[2], 2 * shape[3])


def weight_terms(padded, grad):
    result = lax.conv_general_dilated(
        padded[None],
        grad[None],
        (1, 1, 1),
        "VALID",
        dimension_numbers=("CNDHW", "IODHW", "NCDHW"),
        preferred_element_type=jnp.float32,
    )
    return jnp.transpose(result, (2, 3, 4, 0, 1))


def fine_halo(field):
    return padded_2(field, (("gx", 1), ("gy", 2), ("gz", 3)), 1)


def coarse_halo(field):
    return padded_2(field, (("gx", 1), ("gy", 2), ("gz", 3)), 1)


def on_device(volume, weight_a, bias_a, weight_b, bias_b, cotangent):
    devices_all = lax.axis_size("gx") * lax.axis_size("gy") * lax.axis_size("gz")
    cells_fine = volume.shape[1] * volume.shape[2] * volume.shape[3] * devices_all
    scale_a = 1.0 / math.sqrt(cells_fine)
    scale_b = 1.0 / math.sqrt(cells_fine // 8)
    padded_a = fine_halo(volume)
    before_a = conv_valid(padded_a, weight_a) + bias_a[:, None, None, None]
    pooled = average_pool(activate(before_a)).astype(jnp.bfloat16)
    padded_b = coarse_halo(pooled)
    before_b = conv_valid(padded_b, weight_b) + bias_b[:, None, None, None]
    features_block = activate(before_b).astype(jnp.bfloat16)
    features = lax.all_to_all(features_block, "gz", split_axis=1, concat_axis=3, tiled=True)
    cotangent_block = lax.all_to_all(cotangent, "gz", split_axis=3, concat_axis=1, tiled=True)
    grad_b = (cotangent_block * slope_of(before_b)).astype(jnp.bfloat16)
    grad_pooled = conv_valid(coarse_halo(grad_b), flipped(weight_b)).astype(jnp.bfloat16)
    partial_wb = weight_terms(padded_b, grad_b)
    partial_bb = jnp.sum(grad_b, axis=(1, 2, 3), dtype=jnp.float32)
    grad_a = (spread_back(grad_pooled) * 0.125 * slope_of(before_a)).astype(jnp.bfloat16)
    partial_wa = weight_terms(padded_a, grad_a)
    partial_ba = jnp.sum(grad_a, axis=(1, 2, 3), dtype=jnp.float32)
    grad_input = conv_valid(fine_halo(grad_a), flipped(weight_a)).astype(jnp.bfloat16)
    summed_wa, summed_ba, summed_wb, summed_bb = lax.psum(
        (partial_wa, partial_ba, partial_wb, partial_bb), ("gx", "gy", "gz")
    )
    return (
        features,
        grad_input,
        summed_wa * scale_a,
        summed_ba * scale_a,
        summed_wb * scale_b,
        summed_bb * scale_b,
    )


def solution(mesh):
    return jax.shard_map(
        on_device,
        mesh=mesh,
        in_specs=(P(None, "gx", "gy", "gz"), P(), P(), P(), P(), P(None, ("gx", "gz"), "gy", None)),
        out_specs=(
            P(None, ("gx", "gz"), "gy", None),
            P(None, "gx", "gy", "gz"),
            P(),
            P(),
            P(),
            P(),
        ),
        check_vma=False,
    )
```

profile of v0, /device:TPU:0, one launch (start us, length us, event | category | flops | bytes accessed | tf_op | source)
XLA Modules:
  0.0 355.9 jit_solution(13336533207807933265)
XLA Ops:
  7.2 3.2 fusion.47
  12.7 4.9 %collective-permute-start = (bf16[32,1,8,16]{0,3,2,1:T(8,128)(2,1)S(1)}, bf16[32,1,8,16]{0,3,2,1:T(8,128)(2,1)S(1)}, u32[]{:S(2)}, u32[]{:S(2)}) collective-permute-start(bf16[32,1,8,16]{0,3,2,1:T(8,128)(2,1)S(1)} %copy.155), channel_id=1, source_target_pairs={{0,16},{1,17},{2,18},{3,19},{4,20},{5,21},{6,22},{7,23},{8,24},{9,... | collective-permute-start | bytes 24584 | tf_op jit(solution)/shard_map/ppermute | solution.py:14
  21.7 2.9 collective-permute-done.1
  32.1 3.4 collective-permute-done.5
  38.2 4.9 %copy.125 = bf16[32,34,10,1,8,3]{0,4,5,2,1,3:T(8,128)(2,1)} copy(bf16[32,34,10,1,8,3]{1,0,5,4,2,3:T(8,128)(2,1)} %bitcast.87) | data formatting | bytes 1044480 | tf_op jit(solution)/shard_map/conv_general_dilated | solution.py:32
  44.8 8.3 %multiply_add_fusion = (f32[32,8,8,3,64]{4,2,3,1,0:T(8,128)}, f32[32,8,8,3,64]{4,2,3,1,0:T(8,128)S(1)}) fusion(f32[64]{0:T(128)S(1)} %copy-done.13, bf16[3,3,3,32,64]{4,3,2,1,0:T(8,128)(2,1)S(1)} %copy-done.16, bf16[32,34,10,1,7,2]{0,4,5,2,1,3:T(8,128)(2,1)S(1)} %slice.101, bf16[32,34,10,1,8,3]{0,4,5,2,1,3:T(8,128)(2,1)} %copy.125, ...), kind=kOutput, calls=%fused_computation.17 | convolution fusion | flops 685627392 | bytes 4083480 | tf_op jit(solution)/shard_map/conv_general_dilated | solution.py:32
  58.5 4.2 %collective-permute-done.7 = bf16[64,1,4,8]{0,3,2,1:T(8,128)(2,1)S(1)} collective-permute-done((bf16[64,1,4,8]{0,3,2,1:T(8,128)(2,1)S(1)}, bf16[64,1,4,8]{0,3,2,1:T(8,128)(2,1)S(1)}, u32[]{:S(2)}, u32[]{:S(2)}) %collective-permute-start.7) | collective-permute-done | bytes 4128 | tf_op jit(solution)/shard_map/ppermute | solution.py:17
  64.2 3.6 %collective-permute-start.10 = (bf16[64,18,6,1]{0,3,2,1:T(2,128)(2,1)S(1)}, bf16[64,18,6,1]{0,3,2,1:T(2,128)(2,1)S(1)}, u32[]{:S(2)}, u32[]{:S(2)}) collective-permute-start(bf16[64,18,6,1]{0,3,2,1:T(2,128)(2,1)S(1)} %get-tuple-element.59), channel_id=1, source_target_pairs={{0,1},{1,2},{2,3},{3,4},{4,5},{5,6},{6,7},{7,8},{8,9},{9,10},{10,1... | collective-permute-start | bytes 41480 | tf_op jit(solution)/shard_map/ppermute | solution.py:14
  69.8 9.1 %all-to-all-start.1 = ((bf16[128,1,4,128]{0,2,1,3:T(4,128)(2,1)}), bf16[128,1,4,128]{0,2,1,3:T(4,128)(2,1)S(1)}, u32[]{:S(2)}, u32[]{:S(2)}) async-start(bf16[128,1,4,128]{0,2,1,3:T(4,128)(2,1)} %copy.132), calls=%async_computation.1 | async-start | bytes 262144 | tf_op jit(solution)/shard_map/all_to_all | solution.py:93
  82.0 4.8 %all-to-all-done.1 = bf16[128,1,4,128]{0,2,1,3:T(4,128)(2,1)S(1)} async-done(((bf16[128,1,4,128]{0,2,1,3:T(4,128)(2,1)}), bf16[128,1,4,128]{0,2,1,3:T(4,128)(2,1)S(1)}, u32[]{:S(2)}, u32[]{:S(2)}) %all-to-all-start.1) | async-done | bytes 131104 | tf_op jit(solution)/shard_map/all_to_all | solution.py:93
  91.1 3.4 fusion.55
  94.5 7.7 %copy.142 = bf16[1,32,34,10,18]{1,0,4,3,2:T(2,128)(2,1)} copy(bf16[1,32,34,10,18]{2,1,4,3,0:T(8,128)(2,1)} %fusion.55) | data formatting | bytes 783360 | tf_op jit(solution)/shard_map/broadcast_in_dim | solution.py:33
  102.2 4.1 %copy.141 = f32[32,8,8,3,64]{4,1,3,2,0:T(8,128)} copy(f32[32,8,8,3,64]{4,2,3,1,0:T(8,128)} %get-tuple-element.69) | data formatting | bytes 3145728 | tf_op jit(solution)/shard_map/add | solution.py:28
  106.3 4.2 %all-to-all-start = ((bf16[128,16,4,8]{0,3,2,1:T(8,128)(2,1)}), bf16[128,16,4,8]{0,3,2,1:T(8,128)(2,1)}, u32[]{:S(2)}, u32[]{:S(2)}) async-start(bf16[128,16,4,8]{0,3,2,1:T(8,128)(2,1)} %get-tuple-element.56), calls=%async_computation | async-start | bytes 262144 | tf_op jit(solution)/shard_map/all_to_all | solution.py:92
  115.6 4.1 %fusion.30 = f32[3,3,3,64,128]{4,3,2,1,0:T(8,128)} fusion(bf16[1,64,18,6,10]{1,4,3,2,0:T(8,128)(2,1)S(1)} %copy-done.10, bf16[1,128,16,4,8]{1,4,3,2,0:T(8,128)(2,1)S(1)} %fusion.34), kind=kOutput, calls=%fused_computation.41 | convolution fusion | flops 226492416 | bytes 1154048 | tf_op jit(solution)/shard_map/transpose | solution.py:70
  120.0 2.8 fusion.28
  125.1 5.3 %collective-permute-start.18 = (bf16[64,1,8,16]{0,2,3,1:T(8,128)(2,1)}, bf16[64,1,8,16]{0,2,3,1:T(8,128)(2,1)}, u32[]{:S(2)}, u32[]{:S(2)}) collective-permute-start(bf16[64,1,8,16]{0,2,3,1:T(8,128)(2,1)} %get-tuple-element.52), channel_id=1, source_target_pairs={{0,16},{1,17},{2,18},{3,19},{4,20},{5,21},{6,22},{7,23},{8,24},{9,... | collective-permute-start | bytes 49160 | tf_op jit(solution)/shard_map/ppermute | solution.py:14
  133.3 24.5 %fusion.18 = f32[3,3,3,32,64]{4,3,2,1,0:T(8,128)} fusion(bf16[1,32,34,10,18]{1,0,4,3,2:T(2,128)(2,1)S(1)} %copy-done.8, bf16[1,64,32,8,16]{1,3,4,2,0:T(8,128)(2,1)S(1)} %get-tuple-element.43), kind=kOutput, calls=%fused_computation.27 | convolution fusion | flops 452984832 | bytes 1137152 | tf_op jit(solution)/shard_map/transpose | solution.py:70
  157.8 44.3 %all-reduce = (f32[64]{0:T(128)S(1)}, f32[128]{0:T(128)S(1)}) all-reduce(f32[64]{0:T(128)S(1)} %copy-done.15, f32[128]{0:T(128)S(1)} %copy-done.14), channel_id=1, replica_groups=mesh['gx'=2,'gy'=1,'gz'=16] {'gx','gy','gz'}, use_global_device_ids=true, to_apply=%region_3.0 | all-reduce | flops 192 | bytes 1536 | tf_op jit(solution)/shard_map/psum | solution.py:102
  209.3 3.9 %collective-permute-done.23 = bf16[64,34,10,1]{0,2,3,1:T(8,128)(2,1)S(1)} collective-permute-done((bf16[64,34,10,1]{0,2,3,1:T(8,128)(2,1)S(1)}, bf16[64,34,10,1]{0,2,3,1:T(8,128)(2,1)S(1)}, u32[]{:S(2)}, u32[]{:S(2)}) %collective-permute-start.23) | collective-permute-done | bytes 43552 | tf_op jit(solution)/shard_map/ppermute | solution.py:17
  213.2 3.8 %maximum_bitcast_fusion = bf16[64,34,10,1,18]{0,2,4,1,3:T(8,128)(2,1)S(1)} fusion(bf16[64,34,10,1]{0,2,3,1:T(8,128)(2,1)S(1)} %collective-permute-done.23, bf16[64,34,1,16]{0,2,3,1:T(2,128)(2,1)S(1)} %collective-permute-done.21, bf16[64,1,8,16]{0,2,3,1:T(8,128)(2,1)} %collective-permute-done.19, bf16[64,32,8,16]{0,2,3,1:T(8,128)(2,1)S(1)} %copy-done.3, ...), kind=kLoop, calls=%fused_computation.18 | loop fusion | flops 5483520 | bytes 1566720 | tf_op jit(solution)/shard_map/broadcast_in_dim | solution.py:33
  218.8 11.4 %select_convert_fusion = bf16[32,8,8,3,32]{4,2,3,1,0:T(8,128)(2,1)S(1)} fusion(pred[8,3]{0,1:T(4,128)(4,1)S(1)} %copy-done.19, bf16[3,3,3,32,64]{4,3,2,1,0:T(8,128)(2,1)S(1)} %copy-done.17, bf16[64,34,10,1,7,2]{0,4,5,2,1,3:T(8,128)(2,1)S(1)} %slice.109, bf16[64,34,10,1,8,3]{0,4,5,2,1,3:T(8,128)(2,1)S(1)} %copy.139), kind=kOutput, calls=%fused_computation.16 | convolution fusion | flops 685092864 | bytes 2157592 | tf_op jit(solution)/shard_map/conv_general_dilated | solution.py:32
  230.7 2.9 copy.148
  235.3 109.5 %all-reduce.4.cloned.1.call-done = (f32[3,3,3,32,64]{4,3,2,1,0:T(8,128)}, f32[3,3,3,64,128]{4,3,2,1,0:T(8,128)}) async-done(((f32[3,3,3,32,64]{4,3,2,1,0:T(8,128)}, f32[3,3,3,64,128]{4,3,2,1,0:T(8,128)}), (f32[3,3,3,32,64]{4,3,2,1,0:T(8,128)}, f32[3,3,3,64,128]{4,3,2,1,0:T(8,128)})) %all-reduce.4.cloned.1.call-update) | async-done | bytes 1105936 | tf_op jit(solution)/shard_map/psum | solution.py:102
  (128 shorter events, 59.6 us)
Async XLA Ops:
  12.7 8.1 %collective-permute-start = (bf16[32,1,8,16]{0,3,2,1:T(8,128)(2,1)S(1)}, bf16[32,1,8,16]{0,3,2,1:T(8,128)(2,1)S(1)}, u32[]{:S(2)}, u32[]{:S(2)}) collective-permute-start(bf16[32,1,8,16]{0,3,2,1:T(8,128)(2,1)S(1)} %copy.155), channel_id=1, source_target_pairs={{0,16},{1,17},{2,18},{3,19},{4,20},{5,21},{6,22},{7,23},{8,24},{9,... | collective-permute-start | bytes 24584 | tf_op jit(solution)/shard_map/ppermute | solution.py:14
  18.8 5.8 %collective-permute-start.1 = (bf16[32,1,8,16]{0,3,2,1:T(8,128)(2,1)S(1)}, bf16[32,1,8,16]{0,3,2,1:T(8,128)(2,1)S(1)}, u32[]{:S(2)}, u32[]{:S(2)}) collective-permute-start(bf16[32,1,8,16]{0,3,2,1:T(8,128)(2,1)S(1)} %copy.156), channel_id=1, source_target_pairs={{16,0},{17,1},{18,2},{19,3},{20,4},{21,5},{22,6},{23,7},{24,8},{25... | collective-permute-start | bytes 24584 | tf_op jit(solution)/shard_map/ppermute | solution.py:17
  27.8 1.3 collective-permute-start.2
  29.3 2.8 collective-permute-start.4
  30.6 4.9 %collective-permute-start.5 = (bf16[32,34,10,1]{1,0,3,2:T(8,128)(2,1)S(1)}, bf16[32,34,10,1]{1,0,3,2:T(8,128)(2,1)S(1)}, u32[]{:S(2)}, u32[]{:S(2)}) collective-permute-start(bf16[32,34,10,1]{1,0,3,2:T(8,128)(2,1)S(1)} %get-tuple-element.45), channel_id=1, source_target_pairs={{1,0},{2,1},{3,2},{4,3},{5,4},{6,5},{7,6},{8,7},{9,8},{10,9},{11,1... | collective-permute-start | bytes 65288 | tf_op jit(solution)/shard_map/ppermute | solution.py:17
  55.5 3.0 collective-permute-start.6
  57.1 5.5 %collective-permute-start.7 = (bf16[64,1,4,8]{0,3,2,1:T(8,128)(2,1)S(1)}, bf16[64,1,4,8]{0,3,2,1:T(8,128)(2,1)S(1)}, u32[]{:S(2)}, u32[]{:S(2)}) collective-permute-start(bf16[64,1,4,8]{0,3,2,1:T(8,128)(2,1)S(1)} %get-tuple-element.68), channel_id=1, source_target_pairs={{16,0},{17,1},{18,2},{19,3},{20,4},{21,5},{22,6},{23,7},{24,8},{25... | collective-permute-start | bytes 12296 | tf_op jit(solution)/shard_map/ppermute | solution.py:17
  62.7 1.3 collective-permute-start.8
  64.2 14.8 %collective-permute-start.10 = (bf16[64,18,6,1]{0,3,2,1:T(2,128)(2,1)S(1)}, bf16[64,18,6,1]{0,3,2,1:T(2,128)(2,1)S(1)}, u32[]{:S(2)}, u32[]{:S(2)}) collective-permute-start(bf16[64,18,6,1]{0,3,2,1:T(2,128)(2,1)S(1)} %get-tuple-element.59), channel_id=1, source_target_pairs={{0,1},{1,2},{2,3},{3,4},{4,5},{5,6},{6,7},{7,8},{8,9},{9,10},{10,1... | collective-permute-start | bytes 41480 | tf_op jit(solution)/shard_map/ppermute | solution.py:14
  67.7 11.2 %collective-permute-start.11 = (bf16[64,18,6,1]{0,3,2,1:T(2,128)(2,1)S(1)}, bf16[64,18,6,1]{0,3,2,1:T(2,128)(2,1)S(1)}, u32[]{:S(2)}, u32[]{:S(2)}) collective-permute-start(bf16[64,18,6,1]{0,3,2,1:T(2,128)(2,1)S(1)} %get-tuple-element.60), channel_id=1, source_target_pairs={{1,0},{2,1},{3,2},{4,3},{5,4},{6,5},{7,6},{8,7},{9,8},{10,9},{11,1... | collective-permute-start | bytes 41480 | tf_op jit(solution)/shard_map/ppermute | solution.py:17
  69.8 17.0 %all-to-all-start.1 = ((bf16[128,1,4,128]{0,2,1,3:T(4,128)(2,1)}), bf16[128,1,4,128]{0,2,1,3:T(4,128)(2,1)S(1)}, u32[]{:S(2)}, u32[]{:S(2)}) async-start(bf16[128,1,4,128]{0,2,1,3:T(4,128)(2,1)} %copy.132), calls=%async_computation.1 | async-start | bytes 262144 | tf_op jit(solution)/shard_map/all_to_all | solution.py:93
  88.1 22.4 %collective-permute-start.12 = (bf16[128,1,4,8]{0,3,2,1:T(8,128)(2,1)S(1)}, bf16[128,1,4,8]{0,3,2,1:T(8,128)(2,1)S(1)}, u32[]{:S(2)}, u32[]{:S(2)}) collective-permute-start(bf16[128,1,4,8]{0,3,2,1:T(8,128)(2,1)S(1)} %get-tuple-element.65), channel_id=1, source_target_pairs={{0,16},{1,17},{2,18},{3,19},{4,20},{5,21},{6,22},{7,23},{8,24},{9,... | collective-permute-start | bytes 24584 | tf_op jit(solution)/shard_map/ppermute | solution.py:14
  89.8 20.8 %collective-permute-start.13 = (bf16[128,1,4,8]{0,3,2,1:T(8,128)(2,1)S(1)}, bf16[128,1,4,8]{0,3,2,1:T(8,128)(2,1)S(1)}, u32[]{:S(2)}, u32[]{:S(2)}) collective-permute-start(bf16[128,1,4,8]{0,3,2,1:T(8,128)(2,1)S(1)} %get-tuple-element.66), channel_id=1, source_target_pairs={{16,0},{17,1},{18,2},{19,3},{20,4},{21,5},{22,6},{23,7},{24,8},{25... | collective-permute-start | bytes 24584 | tf_op jit(solution)/shard_map/ppermute | solution.py:17
  106.3 127.2 %all-to-all-start = ((bf16[128,16,4,8]{0,3,2,1:T(8,128)(2,1)}), bf16[128,16,4,8]{0,3,2,1:T(8,128)(2,1)}, u32[]{:S(2)}, u32[]{:S(2)}) async-start(bf16[128,16,4,8]{0,3,2,1:T(8,128)(2,1)} %get-tuple-element.56), calls=%async_computation | async-start | bytes 262144 | tf_op jit(solution)/shard_map/all_to_all | solution.py:92
  110.5 234.3 %all-reduce.4.cloned.1.call-start = ((), (), s32[]{:S(2)}) async-start(), calls=%async_computation.2 | async-start | bytes 2654208 | tf_op jit(solution)/shard_map/psum | solution.py:102
  110.6 1.5 collective-permute-start.14
  112.1 7.6 %collective-permute-start.16 = (bf16[128,18,6,1]{0,3,2,1:T(2,128)(2,1)S(1)}, bf16[128,18,6,1]{0,3,2,1:T(2,128)(2,1)S(1)}, u32[]{:S(2)}, u32[]{:S(2)}) collective-permute-start(bf16[128,18,6,1]{0,3,2,1:T(2,128)(2,1)S(1)} %get-tuple-element.57), channel_id=1, source_target_pairs={{0,1},{1,2},{2,3},{3,4},{4,5},{5,6},{6,7},{7,8},{8,9},{9,10},{10,1... | collective-permute-start | bytes 82952 | tf_op jit(solution)/shard_map/ppermute | solution.py:14
  114.3 5.4 %collective-permute-start.17 = (bf16[128,18,6,1]{0,3,2,1:T(2,128)(2,1)S(1)}, bf16[128,18,6,1]{0,3,2,1:T(2,128)(2,1)S(1)}, u32[]{:S(2)}, u32[]{:S(2)}) collective-permute-start(bf16[128,18,6,1]{0,3,2,1:T(2,128)(2,1)S(1)} %get-tuple-element.58), channel_id=1, source_target_pairs={{1,0},{2,1},{3,2},{4,3},{5,4},{6,5},{7,6},{8,7},{9,8},{10,9},{11,1... | collective-permute-start | bytes 82952 | tf_op jit(solution)/shard_map/ppermute | solution.py:17
  125.1 77.0 %collective-permute-start.18 = (bf16[64,1,8,16]{0,2,3,1:T(8,128)(2,1)}, bf16[64,1,8,16]{0,2,3,1:T(8,128)(2,1)}, u32[]{:S(2)}, u32[]{:S(2)}) collective-permute-start(bf16[64,1,8,16]{0,2,3,1:T(8,128)(2,1)} %get-tuple-element.52), channel_id=1, source_target_pairs={{0,16},{1,17},{2,18},{3,19},{4,20},{5,21},{6,22},{7,23},{8,24},{9,... | collective-permute-start | bytes 49160 | tf_op jit(solution)/shard_map/ppermute | solution.py:14
  130.4 71.7 %collective-permute-start.19 = (bf16[64,1,8,16]{0,2,3,1:T(8,128)(2,1)}, bf16[64,1,8,16]{0,2,3,1:T(8,128)(2,1)}, u32[]{:S(2)}, u32[]{:S(2)}) collective-permute-start(bf16[64,1,8,16]{0,2,3,1:T(8,128)(2,1)} %get-tuple-element.53), channel_id=1, source_target_pairs={{16,0},{17,1},{18,2},{19,3},{20,4},{21,5},{22,6},{23,7},{24,8},{25... | collective-permute-start | bytes 49160 | tf_op jit(solution)/shard_map/ppermute | solution.py:17
  203.4 1.9 collective-permute-start.20
  204.1 1.2 collective-permute-start.21
  206.2 3.1 collective-permute-start.22
  207.5 5.8 %collective-permute-start.23 = (bf16[64,34,10,1]{0,2,3,1:T(8,128)(2,1)S(1)}, bf16[64,34,10,1]{0,2,3,1:T(8,128)(2,1)S(1)}, u32[]{:S(2)}, u32[]{:S(2)}) collective-permute-start(bf16[64,34,10,1]{0,2,3,1:T(8,128)(2,1)S(1)} %get-tuple-element.49), channel_id=1, source_target_pairs={{1,0},{2,1},{3,2},{4,3},{5,4},{6,5},{7,6},{8,7},{9,8},{10,9},{11,1... | collective-permute-start | bytes 130568 | tf_op jit(solution)/shard_map/ppermute | solution.py:17
  (23 other events, 299.0 us)
Sparse Core Ops, SparseCore 0:
  209.4 135.3 all-reduce.3
where the time goes:
time: 362 us; the launch traced here: 356 us
  waiting for transfers between devices  129 us (36%)
  matrix products  53.1 us (15%)
  starting transfers between devices  51.2 us (14%)
  blocking collectives  44.3 us (12%)
  local copies, waits for them, and re-layouts  41 us (11%)
  other arithmetic  22.3 us (6%)
  between operations  15 us (4%)
    psum x1, waiting for transfers between devices, on_device(): lax.psum((partial_wa, partial_ba, partial_wb, partial_bb), ('gx', 'gy', '...  110 us
    psum x1, blocking collectives, on_device(): lax.psum((partial_wa, partial_ba, partial_wb, partial_bb), ('gx', 'gy', '...  44.3 us
    transpose x2, matrix products, weight_terms(): return jnp.transpose(result, (2, 3, 4, 0, 1))  28.6 us
    conv_general_dilated x4, matrix products, conv_valid(): lax.conv_general_dilated(padded[None], weight, (1, 1, 1), 'VALID', dimens...  24.5 us
    ppermute x12, starting transfers between devices, padded_2(): lax.ppermute(lax.slice_in_dim(block, block.shape[dim] - width, None, axis...  24.3 us
    ppermute x12, waiting for transfers between devices, padded_2(): lax.ppermute(lax.slice_in_dim(block, 0, width, axis=dim), axis, backward)  14.5 us
    ppermute x12, starting transfers between devices, padded_2(): lax.ppermute(lax.slice_in_dim(block, 0, width, axis=dim), axis, backward)  13.6 us
    broadcast_in_dim x3, local copies, waits for them, and re-layouts, conv_valid(): padded[None]  10.2 us
  transfers between devices with their start and end apart: 27, of which 6 were waited for; matrix products, arithmetic and copies ran while one was open for 23% of the time, Pallas kernels for 0%

commit v1 on v0

v1 whole, which is shorter than its diff:
```python
import functools
import math

import jax
import jax.numpy as jnp
from jax import lax
from jax.experimental import pallas as pl
from jax.experimental.pallas import tpu as pltpu
from jax.sharding import PartitionSpec as P

LINE = ("gx", "gz")
MESH = pl.DeviceIdType.MESH


def shared(block, axis, dim, width):
    count = lax.axis_size(axis)
    if count == 1:
        edge = jnp.zeros_like(lax.slice_in_dim(block, 0, width, axis=dim))
        return edge, edge
    forward = [(i, i + 1) for i in range(count - 1)]
    backward = [(target, source) for source, target in forward]
    last = block.shape[dim]
    low = lax.ppermute(lax.slice_in_dim(block, last - width, last, axis=dim), axis, forward)
    high = lax.ppermute(lax.slice_in_dim(block, 0, width, axis=dim), axis, backward)
    return low, high


def widened(flat, planes, rows, depth):
    low, high = shared(flat, LINE, 1, rows * depth)
    if lax.axis_size("gy") == 1:
        gap = jnp.zeros((flat.shape[0], depth), flat.dtype)
        pieces = [gap, low, gap]
        for plane in range(planes):
            pieces += [gap, flat[:, plane * rows * depth : (plane + 1) * rows * depth], gap]
        return jnp.concatenate(pieces + [gap, high, gap], axis=1)
    whole = jnp.concatenate([low, flat, high], axis=1)
    whole = whole.reshape(flat.shape[0], planes + 2, rows, depth)
    low, high = shared(whole, "gy", 2, 1)
    return jnp.concatenate([low, whole, high], axis=2).reshape(flat.shape[0], -1)


def slope_of(value):
    sigma = jax.nn.sigmoid(value)
    return sigma + value * sigma * (1.0 - sigma)


def put_windows(wide_ref, windows, planes, rows, depth):
    wide = wide_ref[...]
    width, extent = wide.shape
    place = lax.broadcasted_iota(jnp.int32, (width, extent), 1) % depth
    loose = wide.astype(jnp.float32)
    before = jnp.where(place == 0, 0.0, pltpu.roll(loose, 1, 1)).astype(jnp.bfloat16)
    after = jnp.where(place == depth - 1, 0.0, pltpu.roll(loose, extent - 1, 1)).astype(jnp.bfloat16)
    size = rows * depth
    for third, moved in enumerate((before, wide, after)):
        for first in range(3):
            for second in range(3):
                at = (first * 9 + second * 3 + third) * width
                for plane in range(planes):
                    begin = ((plane + first) * (rows + 2) + second) * depth
                    windows[at : at + width, plane * size : (plane + 1) * size] = moved[
                        :, begin : begin + size
                    ]


def dot_rows(left, right):
    return lax.dot_general(
        left, right, (((1,), (1,)), ((), ())), preferred_element_type=jnp.float32
    )


def forward_a_kernel(dims, wide_ref, weight_ref, bias_ref, pool_ref, before_ref, pooled_ref, windows):
    planes, rows, depth = dims
    put_windows(wide_ref, windows, *dims)
    before = jnp.dot(weight_ref[...], windows[...], preferred_element_type=jnp.float32)
    before = before + bias_ref[...]
    before_ref[...] = before
    active = before * jax.nn.sigmoid(before)
    size = rows * depth
    for row in range(rows // 2):
        parts = [
            active[:, plane * size + (2 * row + j) * depth : plane * size + (2 * row + j + 1) * depth]
            for plane in range(planes)
            for j in range(2)
        ]
        summed = sum(parts[1:], parts[0])
        paired = jnp.dot(
            summed, pool_ref[...], precision=lax.Precision.HIGHEST, preferred_element_type=jnp.float32
        )
        pooled_ref[:, row * depth // 2 : (row + 1) * depth // 2] = (paired * 0.125).astype(jnp.bfloat16)


def middle_kernel(dims, wide_ref, weight_ref, bias_ref, cot_ref, feat_ref, grad_ref, wb_ref, bb_ref, windows):
    put_windows(wide_ref, windows, *dims)
    before = jnp.dot(weight_ref[...], windows[...], preferred_element_type=jnp.float32)
    before = before + bias_ref[...]
    feat_ref[...] = (before * jax.nn.sigmoid(before)).astype(jnp.bfloat16)
    grad = (cot_ref[...].astype(jnp.float32) * slope_of(before)).astype(jnp.bfloat16)
    grad_ref[...] = grad
    wb_ref[...] = dot_rows(windows[...], grad)
    bb_ref[...] = dot_rows(jnp.ones((8, grad.shape[1]), jnp.bfloat16), grad)


def backward_b_kernel(dims, fine, wide_ref, weight_ref, before_ref, spread_ref, grad_ref, windows):
    put_windows(wide_ref, windows, *dims)
    pooled = jnp.dot(weight_ref[...], windows[...], preferred_element_type=jnp.float32)
    pooled = pooled.astype(jnp.bfloat16)
    planes, rows, depth = fine
    size = rows * depth
    for row in range(rows // 2):
        part = pooled[:, row * depth // 2 : (row + 1) * depth // 2]
        spread = jnp.dot(part, spread_ref[...], preferred_element_type=jnp.float32) * 0.125
        for plane in range(planes):
            for j in range(2):
                begin = plane * size + (2 * row + j) * depth
                slope = slope_of(before_ref[:, begin : begin + depth])
                grad_ref[:, begin : begin + depth] = (spread * slope).astype(jnp.bfloat16)


def weight_a_kernel(dims, wide_ref, grad_ref, wa_ref, ba_ref, windows):
    put_windows(wide_ref, windows, *dims)
    grad = grad_ref[...]
    wa_ref[...] = dot_rows(windows[...], grad)
    ba_ref[...] = dot_rows(jnp.ones((8, grad.shape[1]), jnp.bfloat16), grad)


def backward_a_kernel(dims, wide_ref, weight_ref, out_ref, windows):
    put_windows(wide_ref, windows, *dims)
    out = jnp.dot(weight_ref[...], windows[...], preferred_element_type=jnp.float32)
    out_ref[...] = out.astype(jnp.bfloat16)


def local_kernel(body, outs, windows, flops, *operands):
    moved = sum(x.size * x.dtype.itemsize for x in operands)
    return pl.pallas_call(
        body,
        out_shape=[jax.ShapeDtypeStruct(shape, dtype) for shape, dtype in outs],
        in_specs=[pl.BlockSpec(memory_space=pltpu.VMEM)] * len(operands),
        out_specs=[pl.BlockSpec(memory_space=pltpu.VMEM)] * len(outs),
        scratch_shapes=[pltpu.VMEM(windows, jnp.bfloat16)],
        compiler_params=pltpu.CompilerParams(vmem_limit_bytes=48 * 2**20),
        cost_estimate=pl.CostEstimate(flops=flops, bytes_accessed=moved, transcendentals=0),
    )(*operands)


def partner_of(axis, bit):
    me = lax.axis_index(axis)
    mine = (me // bit) % 2
    return me + bit * (1 - 2 * mine), mine


def sum_kernel(steps, halvings, rows, scales, wa_ref, ba_ref, wb_ref, bb_ref, *rest):
    out_wa, out_ba, out_wb, out_bb, acc, gathered, *scratch = rest
    half, width = wa_ref.shape[0] // 2, wa_ref.shape[1]
    top = wb_ref.shape[0]
    count = len(steps)
    sends = scratch[:count]
    recvs = scratch[count : 2 * count]
    sem_send, sem_recv = scratch[2 * count :]
    partners = [partner_of(axis, bit) for axis, bit in steps]
    barrier = pltpu.get_barrier_semaphore()
    for (axis, _), (partner, _) in zip(steps, partners):
        pl.semaphore_signal(barrier, inc=1, device_id={axis: partner}, device_id_type=MESH)
    acc[:top] = wb_ref[...]
    acc[top : top + half, :width] = wa_ref[:half]
    acc[top : top + half, width:] = wa_ref[half:]
    acc[top + half :] = jnp.zeros((rows - top - half, 128), jnp.float32)
    acc[top + half : top + half + 8, :width] = ba_ref[...]
    acc[top + half + 8 : top + half + 16] = bb_ref[...]
    pl.semaphore_wait(barrier, count)
    offset = 0
    size = rows
    kept = []
    for at, ((axis, _), (partner, mine)) in enumerate(zip(steps, partners)):
        source = acc
        if at < halvings:
            size = size // 2
            away = pl.multiple_of(offset + (1 - mine) * size, 16)
            offset = pl.multiple_of(offset + mine * size, 16)
        else:
            away = offset
        sends[at][...] = source[pl.ds(away, size)].astype(jnp.bfloat16)
        copy = pltpu.make_async_remote_copy(
            src_ref=sends[at],
            dst_ref=recvs[at],
            send_sem=sem_send.at[at],
            recv_sem=sem_recv.at[at],
            device_id={axis: partner},
            device_id_type=MESH,
        )
        copy.start()
        copy.wait()
        if at < halvings:
            acc[pl.ds(offset, size)] = source[pl.ds(offset, size)] + recvs[at][...].astype(jnp.float32)
            kept.append((offset, size))
        else:
            acc[pl.ds(offset, size)] = sends[at][...].astype(jnp.float32) + recvs[at][...].astype(jnp.float32)
    gathered[pl.ds(offset, size)] = acc[pl.ds(offset, size)].astype(jnp.bfloat16)
    for back in range(halvings):
        at = halvings - 1 - back
        begin, extent = kept[at]
        (axis, _), (partner, _) = steps[at], partners[at]
        here = gathered.at[pl.ds(begin, extent)]
        copy = pltpu.make_async_remote_copy(
            src_ref=here,
            dst_ref=here,
            send_sem=sem_send.at[count + back],
            recv_sem=sem_recv.at[count + back],
            device_id={axis: partner},
            device_id_type=MESH,
        )
        copy.start()
        copy.wait()
    scale_a, scale_b = scales
    total = gathered[...].astype(jnp.float32)
    out_wb[...] = total[:top] * scale_b
    out_wa[:half] = total[top : top + half, :width] * scale_a
    out_wa[half:] = total[top : top + half, width:] * scale_a
    out_ba[...] = total[top + half : top + half + 1, :width] * scale_a
    out_bb[...] = total[top + half + 8 : top + half + 9] * scale_b


def summed_grads(wa, ba, wb, bb, scales):
    used = wb.shape[0] + wa.shape[0] // 2 + 16
    rows = used + -used % 128
    cut = {
        axis: [2**i for i in range(lax.axis_size(axis).bit_length() - 1)] for axis in ("gz", "gx", "gy")
    }
    steps = [("gz", bit) for bit in cut["gz"][:1]]
    steps += [("gx", bit) for bit in cut["gx"]] + [("gy", bit) for bit in cut["gy"]]
    steps += [("gz", bit) for bit in cut["gz"][1:]]
    halvings = 0
    sizes = []
    size = rows
    for _ in steps:
        if len(sizes) == halvings and size % 32 == 0:
            size //= 2
            halvings += 1
        sizes.append(size)
    buffers = [pltpu.VMEM((s, 128), jnp.bfloat16) for s in sizes]
    total = len(steps) + halvings
    shapes = [wa.shape, (1, ba.shape[1]), wb.shape, (1, bb.shape[1])]
    return pl.pallas_call(
        functools.partial(sum_kernel, steps, halvings, rows, scales),
        out_shape=[jax.ShapeDtypeStruct(shape, jnp.float32) for shape in shapes],
        in_specs=[pl.BlockSpec(memory_space=pltpu.VMEM)] * 4,
        out_specs=[pl.BlockSpec(memory_space=pltpu.VMEM)] * 4,
        scratch_shapes=[
            pltpu.VMEM((rows, 128), jnp.float32),
            pltpu.VMEM((rows, 128), jnp.bfloat16),
            *buffers,
            *buffers,
            pltpu.SemaphoreType.DMA((total,)),
            pltpu.SemaphoreType.DMA((total,)),
        ],
        compiler_params=pltpu.CompilerParams(collective_id=0, has_side_effects=True),
    )(wa, ba, wb, bb)


def outward(weight):
    return weight.reshape(-1, weight.shape[-1]).T


def inward(weight):
    taps = weight[::-1, ::-1, ::-1].reshape(27, *weight.shape[3:])
    return jnp.transpose(taps, (1, 0, 2)).reshape(weight.shape[3], -1)


def on_device(volume, weight_a, bias_a, weight_b, bias_b, cotangent):
    f32, bf16 = jnp.float32, jnp.bfloat16
    count = lax.axis_size("gz")
    devices_all = lax.axis_size("gx") * lax.axis_size("gy") * count
    c1, nx, rows, nz = volume.shape
    cells = nx * rows * nz
    scale_a = 1.0 / math.sqrt(cells * devices_all)
    scale_b = 1.0 / math.sqrt(cells * devices_all // 8)
    c2, c3 = weight_b.shape[3:]
    planes, depth = nx // count, nz * count
    fine = (planes, rows, depth)
    coarse = (planes // 2, rows // 2, depth // 2)
    fewer = cells // 8
    pool = (jnp.arange(depth)[:, None] // 2 == jnp.arange(depth // 2)[None]).astype(f32)
    work_a = 2 * 27 * c1 * c2 * cells
    work_b = 2 * 27 * c2 * c3 * fewer

    slab = lax.all_to_all(volume, "gz", split_axis=1, concat_axis=3, tiled=True).reshape(c1, cells)
    wide_a = widened(slab, *fine)
    before_a, pooled = local_kernel(
        functools.partial(forward_a_kernel, fine),
        [((c2, cells), f32), ((c2, fewer), bf16)],
        (27 * c1, cells),
        work_a,
        wide_a,
        outward(weight_a),
        bias_a[:, None],
        pool,
    )
    wide_b = widened(pooled, *coarse)
    features, grad_b, part_wb, part_bb = local_kernel(
        functools.partial(middle_kernel, coarse),
        [((c3, fewer), bf16), ((c3, fewer), bf16), ((27 * c2, c3), f32), ((8, c3), f32)],
        (27 * c2, fewer),
        2 * work_b,
        wide_b,
        outward(weight_b),
        bias_b[:, None],
        cotangent.reshape(c3, fewer),
    )
    (grad_a,) = local_kernel(
        functools.partial(backward_b_kernel, coarse, fine),
        [((c2, cells), bf16)],
        (27 * c3, fewer),
        work_b,
        widened(grad_b, *coarse),
        inward(weight_b),
        before_a,
        pool.T.astype(bf16),
    )
    part_wa, part_ba = local_kernel(
        functools.partial(weight_a_kernel, fine),
        [((27 * c1, c2), f32), ((8, c2), f32)],
        (27 * c1, cells),
        work_a,
        wide_a,
        grad_a,
    )
    (grad_slab,) = local_kernel(
        functools.partial(backward_a_kernel, fine),
        [((c1, cells), bf16)],
        (27 * c2, cells),
        work_a,
        widened(grad_a, *fine),
        inward(weight_a),
    )
    grad_input = lax.all_to_all(
        grad_slab.reshape(c1, planes, rows, depth), "gz", split_axis=3, concat_axis=1, tiled=True
    )
    sum_wa, sum_ba, sum_wb, sum_bb = summed_grads(
        part_wa, part_ba, part_wb, part_bb, (scale_a, scale_b)
    )
    return (
        features.reshape(cotangent.shape),
        grad_input,
        sum_wa.reshape(weight_a.shape),
        sum_ba.reshape(c2),
        sum_wb.reshape(weight_b.shape),
        sum_bb.reshape(c3),
    )


def solution(mesh):
    return jax.shard_map(
        on_device,
        mesh=mesh,
        in_specs=(P(None, "gx", "gy", "gz"), P(), P(), P(), P(), P(None, ("gx", "gz"), "gy", None)),
        out_specs=(
            P(None, ("gx", "gz"), "gy", None),
            P(None, "gx", "gy", "gz"),
            P(),
            P(),
            P(),
            P(),
        ),
        check_vma=False,
    )
```

time: 362 us -> 141 us (0.39); the launches traced: 356 us -> 140 us
  waiting for transfers between devices: 129 us -> 18.6 us
  matrix products: 53.1 us -> 0 us
  blocking collectives: 44.3 us -> 0 us
  Pallas kernels: 0 us -> 41 us
  other arithmetic: 22.3 us -> 0.12 us
  local copies, waits for them, and re-layouts: 41 us -> 23.3 us
  between operations: 15 us -> 1.24 us
  starting transfers between devices: 51.2 us -> 55.7 us
    psum x1 -> x0, waiting for transfers between devices: 110 us -> none  [on_device(): lax.psum((partial_wa, partial_ba, partial_wb, partial_bb), ('gx', 'gy', '...]
    psum x1 -> x0, blocking collectives: 44.3 us -> none  [on_device(): lax.psum((partial_wa, partial_ba, partial_wb, partial_bb), ('gx', 'gy', '...]
    pallas_call x0 -> x6, Pallas kernels: none -> 41 us  [the longest x1 32.2 us: summed_grads(): pl.pallas_call(functools.partial(sum_kernel, steps, halvings, rows, scale...]
    transpose x2 -> x0, matrix products: 28.6 us -> none  [weight_terms(): return jnp.transpose(result, (2, 3, 4, 0, 1))]
    conv_general_dilated x4 -> x0, matrix products: 24.5 us -> none  [conv_valid(): lax.conv_general_dilated(padded[None], weight, (1, 1, 1), 'VALID', dimens...]
    all_to_all x2, starting transfers between devices: 13.3 us -> 33 us  [the longest x1 25.5 us: on_device(): lax.all_to_all(grad_slab.reshape(c1, planes, rows, depth), 'gz', split_ax...]
    ppermute x24 -> x8, starting transfers between devices: 37.9 us -> 22.8 us  [the longest x4 17.4 us: shared(): lax.ppermute(lax.slice_in_dim(block, last - width, last, axis=dim), axis,...]
    broadcast_in_dim x4 -> x2, local copies, waits for them, and re-layouts: 10.9 us -> 0.21 us  [the longest x1 0.11 us: on_device(): bias_b[:, None]]
  transfers between devices with their start and end apart: 27 -> 10, of which waited for: 6 -> 6; matrix products, arithmetic and copies ran while one was open for 23% -> 3% of each run, Pallas kernels for 0% -> 25%
where the time goes in v1:
time: 141 us; the launch traced here: 140 us
  starting transfers between devices  55.7 us (40%)
  Pallas kernels  41 us (29%)
  local copies, waits for them, and re-layouts  23.3 us (17%)
  waiting for transfers between devices  18.6 us (13%)
    pallas_call x1, Pallas kernels, summed_grads(): pl.pallas_call(functools.partial(sum_kernel, steps, halvings, rows, scale...  32.2 us
    all_to_all x1, starting transfers between devices, on_device(): lax.all_to_all(grad_slab.reshape(c1, planes, rows, depth), 'gz', split_ax...  25.5 us
    ppermute x4, starting transfers between devices, shared(): lax.ppermute(lax.slice_in_dim(block, last - width, last, axis=dim), axis,...  17.4 us
    unnamed x68, local copies, waits for them, and re-layouts  17.3 us
    all_to_all x1, waiting for transfers between devices, on_device(): lax.all_to_all(volume, 'gz', split_axis=1, concat_axis=3, tiled=True)  10 us
    pallas_call x5, Pallas kernels, local_kernel(): pl.pallas_call(body, out_shape=[jax.ShapeDtypeStruct(shape, dtype) for sh...  8.76 us
    ppermute x4, waiting for transfers between devices, shared(): lax.ppermute(lax.slice_in_dim(block, 0, width, axis=dim), axis, backward)  7.46 us
    all_to_all x1, starting transfers between devices, on_device(): lax.all_to_all(volume, 'gz', split_axis=1, concat_axis=3, tiled=True)  7.41 us
  transfers between devices with their start and end apart: 10, of which 6 were waited for; matrix products, arithmetic and copies ran while one was open for 3% of the time, Pallas kernels for 25%

profile of v1, /device:TPU:0, one launch (start us, length us, event | category | flops | bytes accessed | tf_op | source)
XLA Modules:
  0.0 140.0 jit_solution(15007126692871732760)
XLA Ops:
  0.6 3.2 %copy.35 = bf16[32,32,8,16]{0,3,2,1:T(8,128)(2,1)S(1)} copy(bf16[32,32,8,16]{1,3,2,0:T(8,128)(2,1)} %param.6) | data formatting | bytes 524288 | tf_op args[0]
  3.9 1.7 %reshape.106 = bf16[16,2,4096]{2,1,0:T(2,128)(2,1)} reshape(bf16[32,8,16,32]{3,2,1,0:T(8,128)(2,1)S(1)} %bitcast.49) | data formatting | bytes 524288
  5.6 7.4 %all-to-all-start = ((bf16[16,2,4096]{2,1,0:T(2,128)(2,1)}), bf16[16,2,4096]{2,1,0:T(2,128)(2,1)S(1)}, u32[]{:S(2)}, u32[]{:S(2)}) async-start(bf16[16,2,4096]{2,1,0:T(2,128)(2,1)} %reshape.106), calls=%async_computation | async-start | bytes 524288 | tf_op jit(solution)/shard_map/all_to_all | solution.py:286
  13.0 10.0 %all-to-all-done = bf16[16,2,4096]{2,1,0:T(2,128)(2,1)S(1)} async-done(((bf16[16,2,4096]{2,1,0:T(2,128)(2,1)}), bf16[16,2,4096]{2,1,0:T(2,128)(2,1)S(1)}, u32[]{:S(2)}, u32[]{:S(2)}) %all-to-all-start) | async-done | bytes 262176 | tf_op jit(solution)/shard_map/all_to_all | solution.py:286
  24.1 1.8 %collective-permute-start = (bf16[32,2048]{1,0:T(8,128)(2,1)S(1)}, bf16[32,2048]{1,0:T(8,128)(2,1)S(1)}, u32[]{:S(2)}, u32[]{:S(2)}) collective-permute-start(bf16[32,2048]{1,0:T(8,128)(2,1)S(1)} %copy.51), channel_id=1, source_target_pairs={{0,1},{1,2},{2,3},{3,4},{4,5},{5,6},{6,7},{7,8},{8,9},{9,10},{10,1... | collective-permute-start | bytes 393224 | tf_op jit(solution)/shard_map/ppermute | solution.py:23
  26.9 1.3 collective-permute-start.1
  28.3 1.8 %collective-permute-done.1 = bf16[32,2048]{1,0:T(8,128)(2,1)S(1)} collective-permute-done((bf16[32,2048]{1,0:T(8,128)(2,1)S(1)}, bf16[32,2048]{1,0:T(8,128)(2,1)S(1)}, u32[]{:S(2)}, u32[]{:S(2)}) %collective-permute-start.1) | collective-permute-done | bytes 131104 | tf_op jit(solution)/shard_map/ppermute | solution.py:24
  30.1 1.7 %shard_map.109 = (f32[64,4096]{1,0:T(8,128)S(1)}, bf16[64,512]{1,0:T(8,128)(2,1)S(1)}) custom-call(bf16[32,10240]{1,0:T(8,128)(2,1)S(1)} %constant_dynamic-update-slice_fusion.wide_ref, bf16[64,864]{1,0:T(8,128)(2,1)S(1)} %bitcast.45, f32[64,1]{1,0:T(8,128)S(1)} %copy.40.bias_ref, f32[256,128]{1,0:T(8,128)S(1)} %fusion.pool_ref), custom_call_target="tpu_custom_call" | custom-call | flops 452984832 | bytes 897280 | tf_op jit(solution)/shard_map/pallas_call | solution.py:135
  31.8 5.0 %collective-permute-start.2 = (bf16[64,512]{1,0:T(8,128)(2,1)S(1)}, bf16[64,512]{1,0:T(8,128)(2,1)S(1)}, u32[]{:S(2)}, u32[]{:S(2)}) collective-permute-start(bf16[64,512]{1,0:T(8,128)(2,1)S(1)} %get-tuple-element.18), channel_id=1, source_target_pairs={{0,1},{1,2},{2,3},{3,4},{4,5},{5,6},{6,7},{7,8},{8,9},{9,10},{10,1... | collective-permute-start | bytes 196616 | tf_op jit(solution)/shard_map/ppermute | solution.py:23
  36.8 1.3 collective-permute-start.3
  38.2 1.8 %collective-permute-done.3 = bf16[64,512]{1,0:T(8,128)(2,1)S(1)} collective-permute-done((bf16[64,512]{1,0:T(8,128)(2,1)S(1)}, bf16[64,512]{1,0:T(8,128)(2,1)S(1)}, u32[]{:S(2)}, u32[]{:S(2)}) %collective-permute-start.3) | collective-permute-done | bytes 65568 | tf_op jit(solution)/shard_map/ppermute | solution.py:24
  40.0 1.2 shard_map.110
  42.1 4.8 %collective-permute-start.4 = (bf16[128,512]{1,0:T(8,128)(2,1)S(1)}, bf16[128,512]{1,0:T(8,128)(2,1)S(1)}, u32[]{:S(2)}, u32[]{:S(2)}) collective-permute-start(bf16[128,512]{1,0:T(8,128)(2,1)S(1)} %get-tuple-element.20), channel_id=1, source_target_pairs={{0,1},{1,2},{2,3},{3,4},{4,5},{5,6},{6,7},{7,8},{8,9},{9,10},{10,1... | collective-permute-start | bytes 393224 | tf_op jit(solution)/shard_map/ppermute | solution.py:23
  47.4 1.3 collective-permute-start.5
  48.8 1.9 %collective-permute-done.5 = bf16[128,512]{1,0:T(8,128)(2,1)S(1)} collective-permute-done((bf16[128,512]{1,0:T(8,128)(2,1)S(1)}, bf16[128,512]{1,0:T(8,128)(2,1)S(1)}, u32[]{:S(2)}, u32[]{:S(2)}) %collective-permute-start.5) | collective-permute-done | bytes 131104 | tf_op jit(solution)/shard_map/ppermute | solution.py:24
  51.8 5.9 %collective-permute-start.6 = (bf16[64,2048]{1,0:T(8,128)(2,1)S(1)}, bf16[64,2048]{1,0:T(8,128)(2,1)S(1)}, u32[]{:S(2)}, u32[]{:S(2)}) collective-permute-start(bf16[64,2048]{1,0:T(8,128)(2,1)S(1)} %slice.22), channel_id=1, source_target_pairs={{0,1},{1,2},{2,3},{3,4},{4,5},{5,6},{6,7},{7,8},{8,9},{9,10},{10,1... | collective-permute-start | bytes 786440 | tf_op jit(solution)/shard_map/ppermute | solution.py:23
  59.7 1.5 %collective-permute-start.7 = (bf16[64,2048]{1,0:T(8,128)(2,1)}, bf16[64,2048]{1,0:T(8,128)(2,1)}, u32[]{:S(2)}, u32[]{:S(2)}) collective-permute-start(bf16[64,2048]{1,0:T(8,128)(2,1)} %get-tuple-element.50), channel_id=1, source_target_pairs={{1,0},{2,1},{3,2},{4,3},{5,4},{6,5},{7,6},{8,7},{9,8},{10,9},{11,1... | collective-permute-start | bytes 786440 | tf_op jit(solution)/shard_map/ppermute | solution.py:24
  63.1 2.0 %collective-permute-done.7 = bf16[64,2048]{1,0:T(8,128)(2,1)} collective-permute-done((bf16[64,2048]{1,0:T(8,128)(2,1)}, bf16[64,2048]{1,0:T(8,128)(2,1)}, u32[]{:S(2)}, u32[]{:S(2)}) %collective-permute-start.7) | collective-permute-done | bytes 262176 | tf_op jit(solution)/shard_map/ppermute | solution.py:24
  66.1 2.6 %shard_map.112 = bf16[32,4096]{1,0:T(8,128)(2,1)S(1)} custom-call(bf16[64,10240]{1,0:T(8,128)(2,1)S(1)} %constant_dynamic-update-slice_fusion.23.wide_ref, bf16[32,1728]{1,0:T(8,128)(2,1)S(1)} %reshape.100.weight_ref), custom_call_target="tpu_custom_call" | custom-call | flops 452984832 | bytes 1421312 | tf_op jit(solution)/shard_map/pallas_call | solution.py:135
  69.8 1.7 %reshape.108 = bf16[16,2,4096]{2,1,0:T(2,128)(2,1)} reshape(bf16[256,2,8,32]{3,2,1,0:T(8,128)(2,1)S(1)} %bitcast.46) | data formatting | bytes 524288
  71.5 25.5 %all-to-all-start.1 = ((bf16[16,2,4096]{2,1,0:T(2,128)(2,1)}), bf16[16,2,4096]{2,1,0:T(2,128)(2,1)S(1)}, u32[]{:S(2)}, u32[]{:S(2)}) async-start(bf16[16,2,4096]{2,1,0:T(2,128)(2,1)} %reshape.108), calls=%async_computation.1 | async-start | bytes 524288 | tf_op jit(solution)/shard_map/all_to_all | solution.py:335
  97.7 2.2 %shard_map.113 = (f32[864,64]{1,0:T(8,128)S(1)}, f32[8,64]{1,0:T(8,128)S(1)}) custom-call(bf16[32,10240]{1,0:T(8,128)(2,1)S(1)} %constant_dynamic-update-slice_fusion.wide_ref, bf16[64,4096]{1,0:T(8,128)(2,1)S(1)} %shard_map.111.grad_ref), custom_call_target="tpu_custom_call" | custom-call | flops 452984832 | bytes 1179648 | tf_op jit(solution)/shard_map/pallas_call | solution.py:135
  101.3 32.2 %shard_map.114 = (f32[864,64]{1,0:T(8,128)}, f32[1,64]{1,0:T(1,128)}, f32[1728,128]{1,0:T(8,128)}, f32[1,128]{1,0:T(1,128)}) custom-call(f32[864,64]{1,0:T(8,128)} %copy-done.1, f32[8,64]{1,0:T(8,128)} %copy-done.3, f32[1728,128]{1,0:T(8,128)} %copy-done, f32[8,128]{1,0:T(8,128)} %copy-done.2), custom_call_target="tpu_custom_call" | custom-call | tf_op jit(solution)/shard_map/pallas_call | solution.py:243
  134.3 2.9 %copy.49 = bf16[32,32,8,16]{1,3,2,0:T(8,128)(2,1)} copy(bf16[32,32,8,16]{0,3,2,1:T(8,128)(2,1)S(1)} %bitcast.51) | data formatting | bytes 524288
  (93 shorter events, 16.1 us)
Async XLA Ops:
  5.6 17.4 %all-to-all-start = ((bf16[16,2,4096]{2,1,0:T(2,128)(2,1)}), bf16[16,2,4096]{2,1,0:T(2,128)(2,1)S(1)}, u32[]{:S(2)}, u32[]{:S(2)}) async-start(bf16[16,2,4096]{2,1,0:T(2,128)(2,1)} %reshape.106), calls=%async_computation | async-start | bytes 524288 | tf_op jit(solution)/shard_map/all_to_all | solution.py:286
  23.8 2.3 %copy-start.6 = (bf16[3,3,3,32,64]{4,3,2,1,0:T(8,128)(2,1)S(1)}, bf16[3,3,3,32,64]{4,3,2,1,0:T(8,128)(2,1)}, u32[]{:S(2)}) copy-start(bf16[3,3,3,32,64]{4,3,2,1,0:T(8,128)(2,1)} %param.7) | copy-start | bytes 331780
  23.8 2.4 %copy-start.9 = (f32[64]{0:T(128)S(1)}, f32[64]{0:T(128)}, u32[]{:S(2)}) copy-start(f32[64]{0:T(128)} %param.8) | copy-start | bytes 772
  23.8 2.5 %copy-start.4 = (bf16[3,3,3,64,128]{4,3,2,1,0:T(8,128)(2,1)S(1)}, bf16[3,3,3,64,128]{4,3,2,1,0:T(8,128)(2,1)}, u32[]{:S(2)}) copy-start(bf16[3,3,3,64,128]{4,3,2,1,0:T(8,128)(2,1)} %param.9) | copy-start | bytes 1327108
  23.9 2.6 %copy-start.8 = (bf16[128,1,4,128]{3,2,1,0:T(4,128)(2,1)S(1)}, bf16[128,1,4,128]{3,2,1,0:T(4,128)(2,1)}, u32[]{:S(2)}) copy-start(bf16[128,1,4,128]{3,2,1,0:T(4,128)(2,1)} %param.11) | copy-start | bytes 393220
  23.9 2.7 %copy-start.10 = (f32[128]{0:T(128)S(1)}, f32[128]{0:T(128)}, u32[]{:S(2)}) copy-start(f32[128]{0:T(128)} %param.10) | copy-start | bytes 1540
  24.1 4.1 %collective-permute-start = (bf16[32,2048]{1,0:T(8,128)(2,1)S(1)}, bf16[32,2048]{1,0:T(8,128)(2,1)S(1)}, u32[]{:S(2)}, u32[]{:S(2)}) collective-permute-start(bf16[32,2048]{1,0:T(8,128)(2,1)S(1)} %copy.51), channel_id=1, source_target_pairs={{0,1},{1,2},{2,3},{3,4},{4,5},{5,6},{6,7},{7,8},{8,9},{9,10},{10,1... | collective-permute-start | bytes 393224 | tf_op jit(solution)/shard_map/ppermute | solution.py:23
  26.9 3.2 %collective-permute-start.1 = (bf16[32,2048]{1,0:T(8,128)(2,1)S(1)}, bf16[32,2048]{1,0:T(8,128)(2,1)S(1)}, u32[]{:S(2)}, u32[]{:S(2)}) collective-permute-start(bf16[32,2048]{1,0:T(8,128)(2,1)S(1)} %copy.52), channel_id=1, source_target_pairs={{1,0},{2,1},{3,2},{4,3},{5,4},{6,5},{7,6},{8,7},{9,8},{10,9},{11,1... | collective-permute-start | bytes 393224 | tf_op jit(solution)/shard_map/ppermute | solution.py:24
  31.8 6.3 %collective-permute-start.2 = (bf16[64,512]{1,0:T(8,128)(2,1)S(1)}, bf16[64,512]{1,0:T(8,128)(2,1)S(1)}, u32[]{:S(2)}, u32[]{:S(2)}) collective-permute-start(bf16[64,512]{1,0:T(8,128)(2,1)S(1)} %get-tuple-element.18), channel_id=1, source_target_pairs={{0,1},{1,2},{2,3},{3,4},{4,5},{5,6},{6,7},{7,8},{8,9},{9,10},{10,1... | collective-permute-start | bytes 196616 | tf_op jit(solution)/shard_map/ppermute | solution.py:23
  36.8 3.1 %collective-permute-start.3 = (bf16[64,512]{1,0:T(8,128)(2,1)S(1)}, bf16[64,512]{1,0:T(8,128)(2,1)S(1)}, u32[]{:S(2)}, u32[]{:S(2)}) collective-permute-start(bf16[64,512]{1,0:T(8,128)(2,1)S(1)} %get-tuple-element.18), channel_id=1, source_target_pairs={{1,0},{2,1},{3,2},{4,3},{5,4},{6,5},{7,6},{8,7},{9,8},{10,9},{11,1... | collective-permute-start | bytes 196616 | tf_op jit(solution)/shard_map/ppermute | solution.py:24
  41.2 0.9 copy-start
  42.1 5.3 %copy-start.2 = (f32[8,128]{1,0:T(8,128)}, f32[8,128]{1,0:T(8,128)S(1)}, u32[]{:S(2)}) copy-start(f32[8,128]{1,0:T(8,128)S(1)} %get-tuple-element.25.bb_ref) | copy-start | bytes 12292
  42.1 6.7 %collective-permute-start.4 = (bf16[128,512]{1,0:T(8,128)(2,1)S(1)}, bf16[128,512]{1,0:T(8,128)(2,1)S(1)}, u32[]{:S(2)}, u32[]{:S(2)}) collective-permute-start(bf16[128,512]{1,0:T(8,128)(2,1)S(1)} %get-tuple-element.20), channel_id=1, source_target_pairs={{0,1},{1,2},{2,3},{3,4},{4,5},{5,6},{6,7},{7,8},{8,9},{9,10},{10,1... | collective-permute-start | bytes 393224 | tf_op jit(solution)/shard_map/ppermute | solution.py:23
  47.4 3.2 %collective-permute-start.5 = (bf16[128,512]{1,0:T(8,128)(2,1)S(1)}, bf16[128,512]{1,0:T(8,128)(2,1)S(1)}, u32[]{:S(2)}, u32[]{:S(2)}) collective-permute-start(bf16[128,512]{1,0:T(8,128)(2,1)S(1)} %get-tuple-element.20), channel_id=1, source_target_pairs={{1,0},{2,1},{3,2},{4,3},{5,4},{6,5},{7,6},{8,7},{9,8},{10,9},{11,1... | collective-permute-start | bytes 393224 | tf_op jit(solution)/shard_map/ppermute | solution.py:24
  51.8 7.0 %collective-permute-start.6 = (bf16[64,2048]{1,0:T(8,128)(2,1)S(1)}, bf16[64,2048]{1,0:T(8,128)(2,1)S(1)}, u32[]{:S(2)}, u32[]{:S(2)}) collective-permute-start(bf16[64,2048]{1,0:T(8,128)(2,1)S(1)} %slice.22), channel_id=1, source_target_pairs={{0,1},{1,2},{2,3},{3,4},{4,5},{5,6},{6,7},{7,8},{8,9},{9,10},{10,1... | collective-permute-start | bytes 786440 | tf_op jit(solution)/shard_map/ppermute | solution.py:23
  59.7 5.4 %collective-permute-start.7 = (bf16[64,2048]{1,0:T(8,128)(2,1)}, bf16[64,2048]{1,0:T(8,128)(2,1)}, u32[]{:S(2)}, u32[]{:S(2)}) collective-permute-start(bf16[64,2048]{1,0:T(8,128)(2,1)} %get-tuple-element.50), channel_id=1, source_target_pairs={{1,0},{2,1},{3,2},{4,3},{5,4},{6,5},{7,6},{8,7},{9,8},{10,9},{11,1... | collective-permute-start | bytes 786440 | tf_op jit(solution)/shard_map/ppermute | solution.py:24
  71.5 62.0 %all-to-all-start.1 = ((bf16[16,2,4096]{2,1,0:T(2,128)(2,1)}), bf16[16,2,4096]{2,1,0:T(2,128)(2,1)S(1)}, u32[]{:S(2)}, u32[]{:S(2)}) async-start(bf16[16,2,4096]{2,1,0:T(2,128)(2,1)} %reshape.108), calls=%async_computation.1 | async-start | bytes 524288 | tf_op jit(solution)/shard_map/all_to_all | solution.py:335
  99.9 0.8 copy-start.1
  100.7 0.6 copy-start.3
  134.3 2.9 %copy-start.7 = (f32[864,64]{1,0:T(8,128)S(1)}, f32[864,64]{1,0:T(8,128)}, u32[]{:S(2)}) copy-start(f32[864,64]{1,0:T(8,128)} %get-tuple-element.26) | copy-start | bytes 663556
  134.3 3.7 %copy-start.12 = (f32[1,64]{1,0:T(1,128)S(1)}, f32[1,64]{1,0:T(1,128)}, u32[]{:S(2)}) copy-start(f32[1,64]{1,0:T(1,128)} %get-tuple-element.27) | copy-start | bytes 772
  134.3 4.2 %copy-start.5 = (f32[1728,128]{1,0:T(8,128)S(1)}, f32[1728,128]{1,0:T(8,128)}, u32[]{:S(2)}) copy-start(f32[1728,128]{1,0:T(8,128)} %get-tuple-element.28) | copy-start | bytes 2654212
  137.3 2.2 %copy-start.11 = (f32[1,128]{1,0:T(1,128)S(1)}, f32[1,128]{1,0:T(1,128)}, u32[]{:S(2)}) copy-start(f32[1,128]{1,0:T(1,128)} %get-tuple-element.29) | copy-start | bytes 1540
